TPU v7x, 32 devices: a whole 2x2x4 slice. The times are simulated.
32 devices in a mesh: row: 16 (over z, y, core), col: 2 (over x).
Axes of the slice: x: 2, y: 2, z: 4, core: 2. Of those that a mesh axis runs over, the one named last changes fastest.
Arguments:
- layer_input: bfloat16 [16384, 1152], P(('row', 'col')), may hold values from -6 to 6
- attn_gain: bfloat16 [1152], replicated, may hold values from 0.099609375 to 1.8984375
- mlp_gain: bfloat16 [1152], replicated, may hold values from 0.099609375 to 1.8984375
- query_weight: bfloat16 [1152, 1152], P('row', 'col'), may hold values from -0.1875 to 0.1875
- key_weight: bfloat16 [1152, 384], P('row', 'col'), may hold values from -0.1875 to 0.1875
- value_weight: bfloat16 [1152, 384], P('row', 'col'), may hold values from -0.1875 to 0.1875
- out_weight: bfloat16 [1152, 1152], P('col', 'row'), may hold values from -4 to 4
- gate_weight: bfloat16 [1152, 3072], P('row', 'col'), may hold values from -0.1875 to 0.1875
- up_weight: bfloat16 [1152, 3072], P('row', 'col'), may hold values from -0.1875 to 0.1875
- down_weight: bfloat16 [3072, 1152], P('col', 'row'), may hold values from -0.109375 to 0.109375
- seq_ids: int32 [16384], P('row'), may hold values from 0 to 31, as said below
- block_ends: int32 [16384], P('row'), may hold values from 255 to 16383, as said below
- grad_output: bfloat16 [16384, 1152], P(('row', 'col')), may hold values from -6 to 6
Outputs:
- layer_output: bfloat16 [16384, 1152], P(('row', 'col'))
- grad_input: bfloat16 [16384, 1152], P(('row', 'col'))
- grad_attn_gain: float32 [1152], replicated
- grad_mlp_gain: float32 [1152], replicated
- grad_query: float32 [1152, 1152], P('row', 'col')
- grad_key: float32 [1152, 384], P('row', 'col')
- grad_value: float32 [1152, 384], P('row', 'col')
- grad_out_weight: float32 [1152, 1152], P('col', 'row')
- grad_gate: float32 [1152, 3072], P('row', 'col')
- grad_up: float32 [1152, 3072], P('row', 'col')
- grad_down: float32 [3072, 1152], P('col', 'row')
Inputs may be any that keep to these rules, and one draw needn't show every extreme that they name: `seq_ids`: ids never fall; span number s of the aligned spans of 1024 tokens holds exactly two sequences, with ids 2 * s and 2 * s + 1, each of 256 tokens or more. `block_ends`: values never fall; an attention block is a run of 1 to 256 tokens inside one sequence, and the first block of every sequence has exactly 256 tokens.
All inputs are finite; a program needn't handle non-finite values.
Results may differ from a plain program's by a relative error of at most 0.014.
The roundings to bfloat16 on the way count: a program that leaves them out, or rounds other values in their place, can miss the bound.
Values may be sent and summed in bfloat16 or wider, within the bound.
A program may use at most 192 MiB of HBM per device.

v0:
```python
import math
import jax
import jax.numpy as jnp
from jax import lax
from jax.sharding import PartitionSpec as P

QUERY_HEADS = 18
KEY_VALUE_HEADS = 6
HEAD_SIZE_DIM = 64
eps = 1e-05
rope_base = 10000.0
neg_fill = -1e30


def rotate_half(values, head_size):
    lane_index = jnp.arange(values.shape[-1], dtype=jnp.int32) % head_size
    forward_roll = jnp.roll(values, -(head_size // 2), axis=-1)
    backward_roll = jnp.roll(values, head_size // 2, axis=-1)
    return jnp.where(lane_index < head_size // 2, -forward_roll, backward_roll)


def rope_tables(position, table_width, head_size):
    lane_index = (jnp.arange(table_width, dtype=jnp.int32) % (head_size // 2)).astype(jnp.float32)
    frequency = jnp.exp(lane_index * (-2.0 * math.log(rope_base) / head_size))
    angles = position[:, None] * frequency[None, :]
    return (jnp.cos(angles), jnp.sin(angles))


def rotary(values, cosine, sine_part, head_size):
    return values * cosine + rotate_half(values, head_size) * sine_part


def rotary_back(upstream, cosine, sine_part, head_size):
    return upstream * cosine - rotate_half(upstream * sine_part, head_size)


def positions(seq_ids):
    token_index = jnp.arange(seq_ids.shape[0], dtype=jnp.int32)
    earlier = jnp.concatenate([seq_ids[:1] - 1, seq_ids[:-1]])
    seq_start = lax.cummax(jnp.where(seq_ids != earlier, token_index, 0), axis=0)
    return (token_index - seq_start).astype(jnp.float32)


def visible(query_seq, query_end, seq_ids, block_ends):
    return (query_seq[:, None] == seq_ids[None, :]) & (block_ends[None, :] <= query_end[:, None])


def to_rows(values):
    return lax.all_to_all(values, "col", split_axis=0, concat_axis=1, tiled=True)


def to_tokens(values):
    return lax.all_to_all(values, "col", split_axis=1, concat_axis=0, tiled=True)


def col_sums(values):
    return lax.psum_scatter(values, "col", scatter_dimension=0, tiled=True)


def widen(values):
    return lax.all_gather(values, "col", axis=0, tiled=True)


def shards(
    layer_input,
    attn_gain,
    mlp_gain,
    query_weight,
    key_weight,
    value_weight,
    out_weight,
    gate_weight,
    up_weight,
    down_weight,
    seq_ids,
    block_ends,
    grad_output,
):
    col_index = lax.axis_index("col")
    query_rows = layer_input.shape[0]
    block_rows = min(512, query_rows)
    block_count = query_rows // block_rows
    heads_per_group = QUERY_HEADS // KEY_VALUE_HEADS
    group_head_width = heads_per_group * HEAD_SIZE_DIM
    query_width = QUERY_HEADS * HEAD_SIZE_DIM
    score_scale = HEAD_SIZE_DIM ** (-0.5)
    attn_gain_float = attn_gain.astype(jnp.float32)
    mlp_gain_float = mlp_gain.astype(jnp.float32)
    full_input = lax.all_gather(layer_input, "col", axis=0, tiled=True)
    token_rows = full_input.shape[0]
    query_cols, key_cols, value_cols, out_rows, gate_cols, up_cols, down_rows = (
        lax.all_gather(query_weight, "row", axis=0, tiled=True),
        lax.all_gather(key_weight, "row", axis=0, tiled=True),
        lax.all_gather(value_weight, "row", axis=0, tiled=True),
        lax.all_gather(out_weight, "row", axis=1, tiled=True),
        lax.all_gather(gate_weight, "row", axis=0, tiled=True),
        lax.all_gather(up_weight, "row", axis=0, tiled=True),
        lax.all_gather(down_weight, "row", axis=1, tiled=True),
    )
    input_float = full_input.astype(jnp.float32)
    inv_all = lax.rsqrt(jnp.mean(input_float * input_float, axis=1, keepdims=True) + eps)
    attn_in = (input_float * inv_all * attn_gain_float).astype(jnp.bfloat16)
    query_unrotated = jnp.dot(attn_in, query_cols, preferred_element_type=jnp.float32).astype(
        jnp.bfloat16
    )
    key_raw = jnp.dot(attn_in, key_cols, preferred_element_type=jnp.float32).astype(jnp.bfloat16)
    value_projected = jnp.dot(attn_in, value_cols, preferred_element_type=jnp.float32).astype(
        jnp.bfloat16
    )
    query_all = to_rows(query_unrotated)
    key_all, value_all = (
        lax.all_gather(key_raw, "col", axis=1, tiled=True),
        lax.all_gather(value_projected, "col", axis=1, tiled=True),
    )
    position = positions(seq_ids)
    row_start = col_index * query_rows
    query_pos = lax.dynamic_slice_in_dim(position, row_start, query_rows)
    query_seq = lax.dynamic_slice_in_dim(seq_ids, row_start, query_rows)
    query_end = lax.dynamic_slice_in_dim(block_ends, row_start, query_rows)
    query_cos, query_sin = rope_tables(query_pos, query_width, HEAD_SIZE_DIM)
    key_cos, key_sin = rope_tables(position, key_all.shape[1], HEAD_SIZE_DIM)
    query_rotated = (
        rotary(query_all.astype(jnp.float32), query_cos, query_sin, HEAD_SIZE_DIM) * score_scale
    ).astype(jnp.bfloat16)
    key_rotated = rotary(key_all.astype(jnp.float32), key_cos, key_sin, HEAD_SIZE_DIM).astype(
        jnp.bfloat16
    )

    def block_inputs(block_index):
        first_row = block_index * block_rows
        allowed = visible(query_seq, query_end, seq_ids, block_ends)
        return (first_row, allowed)

    def group_scores(query_block, group_index, allowed):
        query_head_rows = lax.dynamic_slice_in_dim(
            query_block, group_index * group_head_width, group_head_width, 1
        ).reshape(block_rows, heads_per_group, HEAD_SIZE_DIM)
        key_group = lax.dynamic_slice_in_dim(
            key_rotated, group_index * HEAD_SIZE_DIM, HEAD_SIZE_DIM, 1
        )
        value_group = lax.dynamic_slice_in_dim(
            value_all, group_index * HEAD_SIZE_DIM, HEAD_SIZE_DIM, 1
        )
        scores = jnp.einsum(
            "qhd,kd->hqk", query_head_rows, key_group, preferred_element_type=jnp.float32
        )
        return (query_head_rows, key_group, value_group, jnp.where(allowed[None], scores, neg_fill))

    def attend_block(block_index):
        first_row, allowed = block_inputs(block_index)

        def attend_head_group(group_index):
            query_head_rows, key_group, value_group, scores = group_scores(
                query_rotated, group_index, allowed
            )
            row_top = jnp.max(scores, axis=2, keepdims=True)
            powers = jnp.exp(scores - row_top)
            exp_total = jnp.sum(powers, axis=2, keepdims=True)
            attn_probs = (powers / exp_total).astype(jnp.bfloat16)
            weighted_values = jnp.einsum(
                "hqk,kd->qhd", attn_probs, value_group, preferred_element_type=jnp.float32
            )
            return (
                weighted_values.reshape(block_rows, group_head_width),
                (row_top + jnp.log(exp_total))[:, :, 0],
            )

        weighted_value_rows, logsumexp_rows = lax.map(
            attend_head_group, jnp.arange(KEY_VALUE_HEADS, dtype=jnp.int32)
        )
        return (
            jnp.transpose(weighted_value_rows, (1, 0, 2)).reshape(block_rows, query_width),
            logsumexp_rows,
        )

    mixed_blocks, log_blocks = lax.map(attend_block, jnp.arange(block_count, dtype=jnp.int32))
    attn_rows = mixed_blocks.reshape(query_rows, query_width).astype(jnp.bfloat16)
    attn_tokens = to_tokens(attn_rows)
    attn_share = col_sums(jnp.dot(attn_tokens, out_rows, preferred_element_type=jnp.float32))
    residual = layer_input.astype(jnp.float32) + attn_share
    inv_two = lax.rsqrt(jnp.mean(residual * residual, axis=1, keepdims=True) + eps)
    normed_two = residual * inv_two
    mlp_in = widen((normed_two * mlp_gain_float).astype(jnp.bfloat16))
    gate_act = jnp.dot(mlp_in, gate_cols, preferred_element_type=jnp.float32)
    up_act = jnp.dot(mlp_in, up_cols, preferred_element_type=jnp.float32)
    hidden = (jax.nn.silu(gate_act) * up_act).astype(jnp.bfloat16)
    mlp_share = col_sums(jnp.dot(hidden, down_rows, preferred_element_type=jnp.float32))
    layer_output = (residual + mlp_share).astype(jnp.bfloat16)
    grad_float = grad_output.astype(jnp.float32)
    grad_full = widen(grad_output)
    grad_down = jnp.einsum("tf,td->fd", hidden, grad_full, preferred_element_type=jnp.float32)
    grad_hidden = jnp.einsum("td,fd->tf", grad_full, down_rows, preferred_element_type=jnp.float32)
    gate_sigmoid = jax.nn.sigmoid(gate_act)
    grad_gate_act = (
        grad_hidden * up_act * gate_sigmoid * (1.0 + gate_act * (1.0 - gate_sigmoid))
    ).astype(jnp.bfloat16)
    grad_up_act = (grad_hidden * gate_act * gate_sigmoid).astype(jnp.bfloat16)
    grad_gate = jnp.einsum("td,tf->df", mlp_in, grad_gate_act, preferred_element_type=jnp.float32)
    grad_up = jnp.einsum("td,tf->df", mlp_in, grad_up_act, preferred_element_type=jnp.float32)
    grad_mlp_share = col_sums(
        jnp.einsum("tf,df->td", grad_gate_act, gate_cols, preferred_element_type=jnp.float32)
        + jnp.einsum("tf,df->td", grad_up_act, up_cols, preferred_element_type=jnp.float32)
    )
    scaled_two = grad_mlp_share * mlp_gain_float
    inner_two = jnp.mean(scaled_two * normed_two, axis=1, keepdims=True)
    grad_residual = grad_float + inv_two * (scaled_two - normed_two * inner_two)
    grad_mlp_gain = jnp.sum(grad_mlp_share * normed_two, axis=0)
    grad_branch = grad_residual.astype(jnp.bfloat16)
    grad_attn_full = widen(grad_branch)
    grad_out_weight = jnp.einsum(
        "tq,td->qd", attn_tokens, grad_attn_full, preferred_element_type=jnp.float32
    )
    grad_mixture = to_rows(
        jnp.einsum(
            "td,qd->tq", grad_attn_full, out_rows, preferred_element_type=jnp.float32
        ).astype(jnp.bfloat16)
    )

    def back_block(carried_state, scan_items):
        block_index, block_log_total = scan_items
        first_row, allowed = block_inputs(block_index)

        def backward_head_group(inner_acc, group_items):
            group_index, log_group = group_items
            keys_acc, values_acc = inner_acc
            query_head_rows, key_group, value_group, scores = group_scores(
                query_rotated, group_index, allowed
            )
            attn_probs = jnp.exp(scores - log_group[:, :, None])
            grad_heads = lax.dynamic_slice_in_dim(
                grad_mixture, group_index * group_head_width, group_head_width, 1
            ).reshape(block_rows, heads_per_group, HEAD_SIZE_DIM)
            grad_probs = jnp.einsum(
                "qhd,kd->hqk", grad_heads, value_group, preferred_element_type=jnp.float32
            )
            value_piece = jnp.einsum(
                "hqk,qhd->kd",
                attn_probs.astype(jnp.bfloat16),
                grad_heads,
                preferred_element_type=jnp.float32,
            )
            inner_dot = jnp.sum(attn_probs * grad_probs, axis=2, keepdims=True)
            grad_scores = (attn_probs * (grad_probs - inner_dot)).astype(jnp.bfloat16)
            query_piece = jnp.einsum(
                "hqk,kd->qhd", grad_scores, key_group, preferred_element_type=jnp.float32
            ).reshape(block_rows, group_head_width)
            key_piece = jnp.einsum(
                "hqk,qhd->kd", grad_scores, query_head_rows, preferred_element_type=jnp.float32
            )
            column = group_index * HEAD_SIZE_DIM
            keys_acc = lax.dynamic_update_slice_in_dim(
                keys_acc,
                lax.dynamic_slice_in_dim(keys_acc, column, HEAD_SIZE_DIM, 1) + key_piece,
                column,
                1,
            )
            values_acc = lax.dynamic_update_slice_in_dim(
                values_acc,
                lax.dynamic_slice_in_dim(values_acc, column, HEAD_SIZE_DIM, 1) + value_piece,
                column,
                1,
            )
            return ((keys_acc, values_acc), query_piece)

        carried_state, query_pieces = lax.scan(
            backward_head_group,
            carried_state,
            (jnp.arange(KEY_VALUE_HEADS, dtype=jnp.int32), block_log_total),
        )
        return (
            carried_state,
            jnp.transpose(query_pieces, (1, 0, 2)).reshape(block_rows, query_width),
        )

    zeros_kv = jnp.zeros((token_rows, key_all.shape[1]), jnp.float32)
    (grad_keys, grad_values), query_blocks = lax.scan(
        back_block, (zeros_kv, zeros_kv), (jnp.arange(block_count, dtype=jnp.int32), log_blocks)
    )
    grad_query_rot = query_blocks.reshape(query_rows, query_width)
    grad_query_raw = to_tokens(
        rotary_back(grad_query_rot * score_scale, query_cos, query_sin, HEAD_SIZE_DIM).astype(
            jnp.bfloat16
        )
    )
    grad_key_part = rotary_back(grad_keys, key_cos, key_sin, HEAD_SIZE_DIM)
    grad_key_sum, grad_value_sum = (
        lax.psum_scatter(grad_key_part, "col", scatter_dimension=1, tiled=True),
        lax.psum_scatter(grad_values, "col", scatter_dimension=1, tiled=True),
    )
    grad_key_raw = grad_key_sum.astype(jnp.bfloat16)
    grad_value_raw = grad_value_sum.astype(jnp.bfloat16)
    grad_query = jnp.einsum(
        "td,tq->dq", attn_in, grad_query_raw, preferred_element_type=jnp.float32
    )
    grad_key = jnp.einsum("td,tq->dq", attn_in, grad_key_raw, preferred_element_type=jnp.float32)
    grad_value = jnp.einsum(
        "td,tq->dq", attn_in, grad_value_raw, preferred_element_type=jnp.float32
    )
    grad_attn_share = col_sums(
        jnp.einsum("tq,dq->td", grad_query_raw, query_cols, preferred_element_type=jnp.float32)
        + jnp.einsum("tq,dq->td", grad_key_raw, key_cols, preferred_element_type=jnp.float32)
        + jnp.einsum("tq,dq->td", grad_value_raw, value_cols, preferred_element_type=jnp.float32)
    )
    own_float = layer_input.astype(jnp.float32)
    inv_one = lax.rsqrt(jnp.mean(own_float * own_float, axis=1, keepdims=True) + eps)
    normed_one = own_float * inv_one
    scaled_one = grad_attn_share * attn_gain_float
    inner_one = jnp.mean(scaled_one * normed_one, axis=1, keepdims=True)
    grad_input = (grad_residual + inv_one * (scaled_one - normed_one * inner_one)).astype(
        jnp.bfloat16
    )
    grad_attn_gain = jnp.sum(grad_attn_share * normed_one, axis=0)
    weight_sums = (
        lax.psum_scatter(grad_query, "row", scatter_dimension=0, tiled=True),
        lax.psum_scatter(grad_key, "row", scatter_dimension=0, tiled=True),
        lax.psum_scatter(grad_value, "row", scatter_dimension=0, tiled=True),
        lax.psum_scatter(grad_out_weight, "row", scatter_dimension=1, tiled=True),
        lax.psum_scatter(grad_gate, "row", scatter_dimension=0, tiled=True),
        lax.psum_scatter(grad_up, "row", scatter_dimension=0, tiled=True),
        lax.psum_scatter(grad_down, "row", scatter_dimension=1, tiled=True),
    )
    gain_sums = lax.psum((grad_attn_gain, grad_mlp_gain), ("row", "col"))
    return (
        layer_output,
        grad_input,
        gain_sums[0],
        gain_sums[1],
        weight_sums[0],
        weight_sums[1],
        weight_sums[2],
        weight_sums[3],
        weight_sums[4],
        weight_sums[5],
        weight_sums[6],
    )


def solution(mesh):
    in_specs = (
        P(("row", "col"), None),
        P(),
        P(),
        P("row", "col"),
        P("row", "col"),
        P("row", "col"),
        P("col", "row"),
        P("row", "col"),
        P("row", "col"),
        P("col", "row"),
        P("row"),
        P("row"),
        P(("row", "col"), None),
    )
    out_specs = (
        P(("row", "col"), None),
        P(("row", "col"), None),
        P(),
        P(),
        P("row", "col"),
        P("row", "col"),
        P("row", "col"),
        P("col", "row"),
        P("row", "col"),
        P("row", "col"),
        P("col", "row"),
    )
    return jax.shard_map(shards, mesh=mesh, in_specs=in_specs, out_specs=out_specs, check_vma=False)
```

profile of v0, /device:TPU:0, one launch (start us, length us, event | category | flops | bytes accessed | tf_op | source)
XLA Modules:
  0.0 1523.2 jit_solution(14034235379282888117)
XLA Ops:
  14.5 24.8 %all_gather.42 = bf16[1152,192]{1,0:T(8,128)(2,1)S(1)} all-gather(bf16[72,192]{1,0:T(8,128)(2,1)S(1)} %copy-done.33), channel_id=1, replica_groups=mesh['row'=16,'col'=2] {'row'}, dimensions={0}, use_global_device_ids=true | all-gather | bytes 470016 | tf_op jit(solution)/shard_map/all_gather | solution.py:93
  39.4 19.0 %all_gather.40 = bf16[1152,192]{1,0:T(8,128)(2,1)S(1)} all-gather(bf16[72,192]{1,0:T(8,128)(2,1)S(1)} %copy-done.34), channel_id=1, replica_groups=mesh['row'=16,'col'=2] {'row'}, dimensions={0}, use_global_device_ids=true | all-gather | bytes 470016 | tf_op jit(solution)/shard_map/all_gather | solution.py:94
  62.2 12.0 all_gather.43
  76.2 11.4 all_gather.41
  99.4 7.6 fusion.73
  107.0 7.4 all-to-all-done
  115.5 11.3 fusion.64
  126.8 62.2 %while.50 = (s32[]{:T(128)}, bf16[6,512,192]{1,2,0:T(8,128)(2,1)S(1)}, f32[6,3,512]{2,1,0:T(4,128)}, s32[6]{0:T(128)S(1)}, bf16[1024,384]{0,1:T(8,128)(2,1)}, /*...) while((s32[]{:T(128)}, ...), condition=%wide.region_6.7_spmd.clone.clone, body=%wide.region_3.6_spmd.clone.sunk.clone | while | flops 418380288 | bytes 22477056 | solution.py:168
  189.0 17.3 %all_to_all.64 = bf16[512,2,576]{0,2,1:T(8,128)(2,1)S(1)} all-to-all(bf16[512,2,576]{0,2,1:T(8,128)(2,1)S(1)} %bitcast.276), channel_id=1, replica_groups=mesh['row'=16,'col'=2] {'col'}, dimensions={1} | all-to-all | bytes 2359296 | tf_op jit(solution)/shard_map/all_to_all | solution.py:53
  206.6 6.2 fusion.124
  214.1 56.8 %reduce-scatter.18.cloned.1.call-done = f32[512,1152]{1,0:T(8,128)} async-done(((f32[1024,1152]{1,0:T(8,128)}), f32[512,1152]{1,0:T(8,128)}) %reduce-scatter.18.cloned.1.call-update) | async-done | bytes 2359312 | tf_op jit(solution)/shard_map/reduce_scatter | solution.py:57
  277.9 42.6 %all-gather.20.cloned.1.call-done = bf16[1152,1536]{1,0:T(8,128)(2,1)} async-done(((bf16[72,1536]{1,0:T(8,128)(2,1)}), bf16[1152,1536]{1,0:T(8,128)(2,1)}) %all-gather.20.cloned.1.call-update) | async-done | bytes 3538960 | tf_op jit(solution)/shard_map/all_gather | solution.py:97
  320.5 37.1 %all-gather.16.cloned.1.call-done = bf16[1024,1152]{1,0:T(8,128)(2,1)} async-done(((bf16[512,1152]{1,0:T(8,128)(2,1)}), bf16[1024,1152]{1,0:T(8,128)(2,1)}) %all-gather.16.cloned.1.call-update) | async-done | bytes 2359312 | tf_op jit(solution)/shard_map/all_gather | solution.py:61
  357.6 9.6 fusion.126
  367.3 40.2 %all-gather.18.cloned.1.call-done = bf16[1152,1536]{1,0:T(8,128)(2,1)} async-done(((bf16[72,1536]{1,0:T(8,128)(2,1)}), bf16[1152,1536]{1,0:T(8,128)(2,1)}) %all-gather.18.cloned.1.call-update) | async-done | bytes 3538960 | tf_op jit(solution)/shard_map/all_gather | solution.py:96
  407.4 9.7 fusion.125
  417.1 27.0 %all-gather.24.cloned.1.call-done = bf16[1024,1152]{1,0:T(8,128)(2,1)} async-done(((bf16[512,1152]{1,0:T(8,128)(2,1)}), bf16[1024,1152]{1,0:T(8,128)(2,1)}) %all-gather.24.cloned.1.call-update) | async-done | bytes 2359312 | tf_op jit(solution)/shard_map/all_gather | solution.py:61
  444.1 49.8 %all-gather.22.cloned.1.call-done = bf16[1536,1152]{0,1:T(8,128)(2,1)} async-done(((bf16[1536,72]{0,1:T(8,128)(2,1)}), bf16[1536,1152]{0,1:T(8,128)(2,1)}) %all-gather.22.cloned.1.call-update) | async-done | bytes 3538960 | tf_op jit(solution)/shard_map/all_gather | solution.py:98
  493.9 12.5 multiply_convert_fusion
  510.7 6.0 convolution_add_fusion.2
  516.8 59.1 %reduce-scatter.22.cloned.1.call-done = f32[512,1152]{1,0:T(8,128)} async-done(((f32[1024,1152]{1,0:T(8,128)}), f32[512,1152]{1,0:T(8,128)}) %reduce-scatter.22.cloned.1.call-update) | async-done | bytes 2359312 | tf_op jit(solution)/shard_map/reduce_scatter | solution.py:57
  581.8 36.2 %all-gather.26.cloned.1.call-done = bf16[1024,1152]{1,0:T(8,128)(2,1)} async-done(((bf16[512,1152]{1,0:T(8,128)(2,1)}), bf16[1024,1152]{1,0:T(8,128)(2,1)}) %all-gather.26.cloned.1.call-update) | async-done | bytes 2359312 | tf_op jit(solution)/shard_map/all_gather | solution.py:61
  623.0 4.4 all-to-all-start.2
  627.7 15.1 all-to-all-done.2
  645.5 125.0 %while.51 = (s32[]{:T(128)}, f32[1024,384]{0,1:T(8,128)}, f32[1024,384]{0,1:T(8,128)}, f32[6,512,192]{1,2,0:T(8,128)}, s32[6]{0:T(128)S(1)}, /*index=5*/bf16[102...) while((s32[]{:T(128)}, f32[1024,384]{0,1:T(8,128)}, ...), condition=%wide.region_15.16_spmd.clone.clone, body=%wide.region_13.15_spmd.clone.sunk.clone | while | flops 1027209728 | bytes 55630144 | solution.py:265
  770.5 6.5 fusion.70
  778.4 6.8 fusion.74
  786.3 8.0 fusion.51
  796.7 8.7 subtract_convert_fusion
  805.4 18.5 %all_to_all.65 = bf16[512,2,576]{0,2,1:T(8,128)(2,1)S(1)} all-to-all(bf16[512,2,576]{0,2,1:T(8,128)(2,1)S(1)} %subtract_convert_fusion), channel_id=1, replica_groups=mesh['row'=16,'col'=2] {'col'}, dimensions={1} | all-to-all | bytes 2359296 | tf_op jit(solution)/shard_map/all_to_all | solution.py:53
  828.4 5.7 convolution_add_fusion.1
  834.1 6.9 reduce-scatter.26.cloned.1.call-done
  841.0 5.6 convolution_add_fusion
  846.7 9.4 fusion.127
  857.7 7.7 fusion.133
  867.1 7.6 fusion.132
  874.7 7.9 fusion.131
  883.9 5.4 fusion.130
  909.8 40.1 %all-reduce.2 = (f32[1152]{0:T(1024)}, f32[1152]{0:T(1024)}) all-reduce(f32[1152]{0:T(1024)} %get-tuple-element.251, f32[1152]{0:T(1024)} %get-tuple-element.249), channel_id=1, replica_groups=mesh['row'=16,'col'=2] {'row','col'}, use_global_device_ids=true, to_apply=%region_21.22 | all-reduce | flops 2304 | bytes 18432 | tf_op jit(solution)/shard_map/psum | solution.py:322
  951.1 19.2 %reduce-scatter.20.cloned.1.call-done = f32[512,1152]{1,0:T(8,128)} async-done(((f32[1024,1152]{1,0:T(8,128)}), f32[512,1152]{1,0:T(8,128)}) %reduce-scatter.20.cloned.1.call-update) | async-done | bytes 2359312 | tf_op jit(solution)/shard_map/reduce_scatter | solution.py:57
  970.3 5.1 fusion.60
  975.4 89.2 %reduce-scatter.38.cloned.1.call-done = f32[1536,72]{0,1:T(8,128)} async-done(((f32[1536,1152]{0,1:T(8,128)}), f32[1536,72]{0,1:T(8,128)}) %reduce-scatter.38.cloned.1.call-update) | async-done | bytes 442384 | tf_op jit(solution)/shard_map/reduce_scatter | solution.py:320
  1064.7 94.5 %reduce-scatter.36.cloned.1.call-done = f32[72,1536]{1,0:T(8,128)} async-done(((f32[1152,1536]{1,0:T(8,128)}), f32[72,1536]{1,0:T(8,128)}) %reduce-scatter.36.cloned.1.call-update) | async-done | bytes 442384 | tf_op jit(solution)/shard_map/reduce_scatter | solution.py:319
  1159.2 94.0 %reduce-scatter.34.cloned.1.call-done = f32[72,1536]{1,0:T(8,128)} async-done(((f32[1152,1536]{1,0:T(8,128)}), f32[72,1536]{1,0:T(8,128)}) %reduce-scatter.34.cloned.1.call-update) | async-done | bytes 442384 | tf_op jit(solution)/shard_map/reduce_scatter | solution.py:318
  1253.3 69.9 %reduce-scatter.42.cloned.1.call-done = f32[576,72]{0,1:T(8,128)} async-done(((f32[576,1152]{0,1:T(8,128)}), f32[576,72]{0,1:T(8,128)}) %reduce-scatter.42.cloned.1.call-update) | async-done | bytes 165904
  1323.1 61.6 %reduce-scatter.32.cloned.1.call-done = f32[72,192]{1,0:T(8,128)} async-done(((f32[1152,192]{1,0:T(8,128)}), f32[72,192]{1,0:T(8,128)}) %reduce-scatter.32.cloned.1.call-update) | async-done | bytes 55312 | tf_op jit(solution)/shard_map/reduce_scatter | solution.py:316
  1384.8 61.8 %reduce-scatter.30.cloned.1.call-done = f32[72,192]{1,0:T(8,128)} async-done(((f32[1152,192]{1,0:T(8,128)}), f32[72,192]{1,0:T(8,128)}) %reduce-scatter.30.cloned.1.call-update) | async-done | bytes 55312 | tf_op jit(solution)/shard_map/reduce_scatter | solution.py:315
  1446.6 69.3 %reduce-scatter.40.cloned.1.call-done = f32[72,576]{1,0:T(8,128)} async-done(((f32[1152,576]{1,0:T(8,128)}), f32[72,576]{1,0:T(8,128)}) %reduce-scatter.40.cloned.1.call-update) | async-done | bytes 165904
  (342 shorter events, 258.2 us)
Async XLA Ops:
  7.2 7.3 copy-start.41
  7.2 7.3 copy-start.33
  7.2 32.2 %copy-start.34 = (bf16[72,192]{1,0:T(8,128)(2,1)S(1)}, bf16[72,192]{1,0:T(8,128)(2,1)}, u32[]{:S(2)}) copy-start(bf16[72,192]{1,0:T(8,128)(2,1)} %param.22) | copy-start | bytes 82948
  7.2 51.2 %all-gather.10.cloned.1.call-start = ((), (), s32[]{:S(2)}) async-start(), calls=%async_computation.17 | async-start | bytes 3538944 | tf_op jit(solution)/shard_map/all_gather | solution.py:89
  8.0 82.0 %all-gather.12.cloned.1.call-start = ((), (), s32[]{:S(2)}) async-start(), calls=%async_computation.18 | async-start | bytes 1566720 | tf_op jit(solution)/shard_map/all_gather | solution.py:92
  8.7 197.8 %all-gather.14.cloned.1.call-start = ((), (), s32[]{:S(2)}) async-start(), calls=%async_computation.19 | async-start | bytes 1566720 | tf_op jit(solution)/shard_map/all_gather | solution.py:95
  13.9 47.0 %copy-start.24 = (f32[1024]{0:T(1024)}, f32[1024]{0:T(1024)S(1)}, u32[]{:S(2)}) copy-start(f32[1024]{0:T(1024)S(1)} %fusion.97) | copy-start | bytes 12292
  14.5 46.4 %copy-start.27 = (f32[1152]{0:T(1024)}, f32[1152]{0:T(1024)S(1)}, u32[]{:S(2)}) copy-start(f32[1152]{0:T(1024)S(1)} %convert_element_type.125) | copy-start | bytes 13828
  39.4 22.8 %copy-start.15 = (bf16[1152,192]{1,0:T(8,128)(2,1)}, bf16[1152,192]{1,0:T(8,128)(2,1)S(1)}, u32[]{:S(2)}) copy-start(bf16[1152,192]{1,0:T(8,128)(2,1)S(1)} %all_gather.42) | copy-start | bytes 1327108
  58.4 15.9 %copy-start.13 = (bf16[1152,192]{1,0:T(8,128)(2,1)}, bf16[1152,192]{1,0:T(8,128)(2,1)S(1)}, u32[]{:S(2)}) copy-start(bf16[1152,192]{1,0:T(8,128)(2,1)S(1)} %all_gather.40) | copy-start | bytes 1327108
  61.0 13.3 copy-start.43
  74.3 15.7 %copy-start.28 = (f32[1152]{0:T(1024)S(1)}, f32[1152]{0:T(1024)}, u32[]{:S(2)}) copy-start(f32[1152]{0:T(1024)} %copy-done.27) | copy-start | bytes 13828
  95.1 19.3 %all-to-all-start = ((bf16[2,512,576]{1,2,0:T(8,128)(2,1)}), bf16[2,512,576]{1,2,0:T(8,128)(2,1)S(1)}, u32[]{:S(2)}, u32[]{:S(2)}) async-start(bf16[2,512,576]{1,2,0:T(8,128)(2,1)} %bitcast.277), calls=%async_computation | async-start | bytes 2359296 | tf_op jit(solution)/shard_map/all_to_all | solution.py:49
  98.7 172.2 %reduce-scatter.18.cloned.1.call-start = ((), (), s32[]{:S(2)}) async-start(), calls=%async_computation.20 | async-start | bytes 7077888 | tf_op jit(solution)/shard_map/reduce_scatter | solution.py:57
  206.5 6.3 copy-start.17
  212.8 58.1 %copy-start.7 = (bf16[512,1152]{1,0:T(8,128)(2,1)S(1)}, bf16[512,1152]{1,0:T(8,128)(2,1)}, u32[]{:S(2)}) copy-start(bf16[512,1152]{1,0:T(8,128)(2,1)} %param.17) | copy-start | bytes 3538948
  212.8 107.7 %all-gather.20.cloned.1.call-start = ((), (), s32[]{:S(2)}) async-start(), calls=%async_computation.23 | async-start | bytes 3760128 | tf_op jit(solution)/shard_map/all_gather | solution.py:97
  213.4 144.2 %all-gather.16.cloned.1.call-start = ((), (), s32[]{:S(2)}) async-start(), calls=%async_computation.21 | async-start | bytes 3538944 | tf_op jit(solution)/shard_map/all_gather | solution.py:61
  273.7 305.2 %copy-start.1 = (f32[512,1152]{1,0:T(8,128)}, f32[512,1152]{1,0:T(8,128)S(1)}, u32[]{:S(2)}) copy-start(f32[512,1152]{1,0:T(8,128)S(1)} %get-tuple-element.306) | copy-start | bytes 7077892
  275.3 132.2 %all-gather.18.cloned.1.call-start = ((), (), s32[]{:S(2)}) async-start(), calls=%async_computation.22 | async-start | bytes 3760128 | tf_op jit(solution)/shard_map/all_gather | solution.py:96
  276.0 168.1 %all-gather.24.cloned.1.call-start = ((), (), s32[]{:S(2)}) async-start(), calls=%async_computation.26 | async-start | bytes 3538944 | tf_op jit(solution)/shard_map/all_gather | solution.py:61
  276.8 217.1 %all-gather.22.cloned.1.call-start = ((), (), s32[]{:S(2)}) async-start(), calls=%async_computation.24 | async-start | bytes 3760128 | tf_op jit(solution)/shard_map/all_gather | solution.py:98
  277.5 298.4 %reduce-scatter.22.cloned.1.call-start = ((), (), s32[]{:S(2)}) async-start(), calls=%async_computation.27 | async-start | bytes 7077888 | tf_op jit(solution)/shard_map/reduce_scatter | solution.py:57
  493.9 12.5 copy-start.48
  516.7 62.8 %copy-start.9 = (bf16[512,1152]{1,0:T(8,128)(2,1)S(1)}, bf16[512,1152]{1,0:T(8,128)(2,1)}, u32[]{:S(2)}) copy-start(bf16[512,1152]{1,0:T(8,128)(2,1)} %param.29) | copy-start | bytes 3538948
  516.7 101.3 %all-gather.26.cloned.1.call-start = ((), (), s32[]{:S(2)}) async-start(), calls=%async_computation.28 | async-start | bytes 3538944 | tf_op jit(solution)/shard_map/all_gather | solution.py:61
  623.0 19.8 %all-to-all-start.2 = ((bf16[2,512,576]{1,2,0:T(8,128)(2,1)}), bf16[2,512,576]{1,2,0:T(8,128)(2,1)}, u32[]{:S(2)}, u32[]{:S(2)}) async-start(bf16[2,512,576]{1,2,0:T(8,128)(2,1)} %bitcast.162), calls=%async_computation.5 | async-start | bytes 2359296 | tf_op jit(solution)/shard_map/all_to_all | solution.py:49
  627.4 201.0 %reduce-scatter.24.cloned.1.call-start = ((), (), s32[]{:S(2)}) async-start(), calls=%async_computation.29 | async-start | bytes 2359296 | tf_op jit(solution)/shard_map/reduce_scatter | solution.py:287
  645.5 125.0 %copy-start.26 = (f32[1024]{0:T(1024)S(1)}, f32[1024]{0:T(1024)}, u32[]{:S(2)}) copy-start(f32[1024]{0:T(1024)} %copy-done.24) | copy-start | bytes 12292
  645.5 125.0 %copy-start.36 = (f32[384]{0:T(512)S(1)}, f32[384]{0:T(512)}, u32[]{:S(2)}) copy-start(f32[384]{0:T(512)} %fusion.100) | copy-start | bytes 4612
  691.7 5.4 copy-start
  712.5 5.4 copy-start
  778.4 7.2 copy-start.12
  785.3 55.7 %reduce-scatter.26.cloned.1.call-start = ((), (), s32[]{:S(2)}) async-start(), calls=%async_computation.30 | async-start | bytes 2359296 | tf_op jit(solution)/shard_map/reduce_scatter | solution.py:288
  786.3 8.0 copy-start.4
  794.4 112.4 %reduce-scatter.28.cloned.1.call-start = ((), (), s32[]{:S(2)}) async-start(), calls=%async_computation.31 | async-start | bytes 7077888 | tf_op jit(solution)/shard_map/reduce_scatter | solution.py:57
  805.4 18.7 %copy-start.51 = (bf16[1152,576]{1,0:T(8,128)(2,1)S(1)}, bf16[1152,576]{1,0:T(8,128)(2,1)}, u32[]{:S(2)}) copy-start(bf16[1152,576]{1,0:T(8,128)(2,1)} %all-gather.12.cloned.1.call-done) | copy-start | bytes 3981316
  828.4 12.6 copy-start.14
  846.7 123.7 %reduce-scatter.20.cloned.1.call-start = ((), (), s32[]{:S(2)}) async-start(), calls=%async_computation.25 | async-start | bytes 7077888 | tf_op jit(solution)/shard_map/reduce_scatter | solution.py:57
  856.1 208.6 %reduce-scatter.38.cloned.1.call-start = ((), (), s32[]{:S(2)}) async-start(), calls=%async_computation.36 | async-start | bytes 7520256 | tf_op jit(solution)/shard_map/reduce_scatter | solution.py:320
  865.4 293.8 %reduce-scatter.36.cloned.1.call-start = ((), (), s32[]{:S(2)}) async-start(), calls=%async_computation.35 | async-start | bytes 7520256 | tf_op jit(solution)/shard_map/reduce_scatter | solution.py:319
  874.7 378.6 %reduce-scatter.34.cloned.1.call-start = ((), (), s32[]{:S(2)}) async-start(), calls=%async_computation.34 | async-start | bytes 7520256 | tf_op jit(solution)/shard_map/reduce_scatter | solution.py:318
  882.6 440.5 %reduce-scatter.42.cloned.1.call-start = ((), (), s32[]{:S(2)}) async-start(), calls=%async_computation.38 | async-start | bytes 3133440
  889.3 495.4 %reduce-scatter.32.cloned.1.call-start = ((), (), s32[]{:S(2)}) async-start(), calls=%async_computation.33 | async-start | bytes 1253376 | tf_op jit(solution)/shard_map/reduce_scatter | solution.py:316
  894.2 552.4 %reduce-scatter.30.cloned.1.call-start = ((), (), s32[]{:S(2)}) async-start(), calls=%async_computation.32 | async-start | bytes 1253376 | tf_op jit(solution)/shard_map/reduce_scatter | solution.py:315
  897.5 618.4 %reduce-scatter.40.cloned.1.call-start = ((), (), s32[]{:S(2)}) async-start(), calls=%async_computation.37 | async-start | bytes 3133440
  901.6 68.7 %copy-start.2 = (f32[512,1152]{1,0:T(8,128)S(1)}, f32[512,1152]{1,0:T(8,128)}, u32[]{:S(2)}) copy-start(f32[512,1152]{1,0:T(8,128)} %copy-done.1) | copy-start | bytes 7077892
  901.6 68.7 %copy-start.23 = (f32[1152]{0:T(1024)S(1)}, f32[1152]{0:T(1024)}, u32[]{:S(2)}) copy-start(f32[1152]{0:T(1024)} %convert_element_type.142) | copy-start | bytes 13828
  (35 other events, 89.4 us)
Sparse Core Ops, SparseCore 0:
  9.6 38.7 all-gather.9
  50.6 39.3 all-gather.11
  92.1 38.1 all-gather.13
  212.9 57.8 reduce-scatter.17
  273.3 47.1 all-gather.19
  322.5 35.0 all-gather.15
  360.2 47.1 all-gather.17
  409.0 35.0 all-gather.23
  446.7 47.1 all-gather.21
  516.8 58.9 reduce-scatter.21
  582.0 36.0 all-gather.25
  785.4 26.4 reduce-scatter.23
  814.2 26.7 reduce-scatter.25
  846.8 59.9 reduce-scatter.27
  909.1 61.2 reduce-scatter.19
  974.8 89.8 reduce-scatter.37
  1069.6 89.5 reduce-scatter.35
  1163.7 89.5 reduce-scatter.33
  1258.3 64.8 reduce-scatter.41
  1327.6 57.0 reduce-scatter.31
  1389.4 57.1 reduce-scatter.29
  1451.6 64.2 reduce-scatter.39
where the time goes:
time: 1530 us; the launch traced here: 1520 us
  waiting for transfers between devices  949 us (62%)
  matrix products  228 us (15%)
  blocking collectives  143 us (9%)
  other arithmetic  115 us (8%)
  local copies, waits for them, and re-layouts  45.7 us (3%)
  loops' own time  16.1 us (1%)
  between operations  16.1 us (1%)
    unnamed x24, waiting for transfers between devices  144 us
    reduce_scatter x4, waiting for transfers between devices, col_sums(): return lax.psum_scatter(values, 'col', scatter_dimension=0, tiled=True)  139 us
    all_gather x3, waiting for transfers between devices, widen(): return lax.all_gather(values, 'col', axis=0, tiled=True)  100 us
    reduce_scatter x1, waiting for transfers between devices, shards(): lax.psum_scatter(grad_up, 'row', scatter_dimension=0, tiled=True)  94.5 us
    reduce_scatter x1, waiting for transfers between devices, shards(): lax.psum_scatter(grad_gate, 'row', scatter_dimension=0, tiled=True)  94 us
    reduce_scatter x1, waiting for transfers between devices, shards(): lax.psum_scatter(grad_down, 'row', scatter_dimension=1, tiled=True)  89.2 us
    reduce_scatter x1, waiting for transfers between devices, shards(): lax.psum_scatter(grad_key, 'row', scatter_dimension=0, tiled=True)  61.8 us
    reduce_scatter x1, waiting for transfers between devices, shards(): lax.psum_scatter(grad_value, 'row', scatter_dimension=0, tiled=True)  61.6 us
  transfers between devices with their start and end apart: 24, of which 21 were waited for; matrix products, arithmetic and copies ran while one was open for 13% of the time, Pallas kernels for 0%

commit v1 on v0

--- a/solution.py
+++ b/solution.py
@@ -12,6 +12,28 @@
 neg_fill = -1e30
 
 
+def laid_out(tiles, dim):
+    shape = list(tiles.shape[1:])
+    shape[dim] *= tiles.shape[0]
+    return jnp.moveaxis(tiles, 0, dim).reshape(shape)
+
+
+def grow_blocks(array, axis):
+    devices = lax.axis_size(axis)
+    tiles = array[None]
+    for level in range(devices.bit_length() - 1):
+        distance = 1 << level
+        other = lax.ppermute(tiles, axis, [(i, i ^ distance) for i in range(devices)])
+        both = jnp.stack([tiles, other])
+        upper = lax.axis_index(axis) >> level & 1
+        tiles = jnp.where(upper == 0, both, both[::-1]).reshape(-1, *array.shape)
+    return tiles
+
+
+def doubled_up(x, axis, dim):
+    return laid_out(grow_blocks(x, axis), dim)
+
+
 def rotate_half(values, head_size):
     lane_index = jnp.arange(values.shape[-1], dtype=jnp.int32) % head_size
     forward_roll = jnp.roll(values, -(head_size // 2), axis=-1)
@@ -58,7 +80,7 @@
 
 
 def widen(values):
-    return lax.all_gather(values, "col", axis=0, tiled=True)
+    return doubled_up(values, "col", 0)
 
 
 def shards(

time: 1530 us -> 1460 us (0.954)
  waiting for transfers between devices: 949 us -> 876 us
  matrix products: 228 us -> 212 us
    all_gather x3 -> x0, waiting for transfers between devices: 100 us -> none  [widen(): return lax.all_gather(values, 'col', axis=0, tiled=True)]
    reduce_scatter x4, waiting for transfers between devices: 139 us -> 201 us  [col_sums(): return lax.psum_scatter(values, 'col', scatter_dimension=0, tiled=True)]
    ppermute x0 -> x3, waiting for transfers between devices: none -> 53.1 us  [grow_blocks(): lax.ppermute(tiles, axis, [(i, i ^ distance) for i in range(devices)])]
    reduce_scatter x1, waiting for transfers between devices: 94 us -> 48.4 us  [shards(): lax.psum_scatter(grad_gate, 'row', scatter_dimension=0, tiled=True)]
    all_gather x1, waiting for transfers between devices: 40.2 us -> 10.6 us  [shards(): lax.all_gather(gate_weight, 'row', axis=0, tiled=True)]
    unnamed x24 -> x21, waiting for transfers between devices: 144 us -> 143 us
  transfers between devices with their start and end apart: 24 -> 24, of which waited for: 21 -> 20; matrix products, arithmetic and copies ran while one was open for 13% -> 14% of each run, Pallas kernels for 0% -> 0%
where the time goes in v1:
time: 1460 us; the launch traced here: 1450 us
  waiting for transfers between devices  876 us (60%)
  matrix products  212 us (15%)
  blocking collectives  143 us (10%)
  other arithmetic  122 us (8%)
  local copies, waits for them, and re-layouts  53.9 us (4%)
  loops' own time  16.2 us (1%)
  between operations  15.8 us (1%)
    reduce_scatter x4, waiting for transfers between devices, col_sums(): return lax.psum_scatter(values, 'col', scatter_dimension=0, tiled=True)  201 us
    unnamed x21, waiting for transfers between devices  143 us
    reduce_scatter x1, waiting for transfers between devices, shards(): lax.psum_scatter(grad_up, 'row', scatter_dimension=0, tiled=True)  94.6 us
    reduce_scatter x1, waiting for transfers between devices, shards(): lax.psum_scatter(grad_down, 'row', scatter_dimension=1, tiled=True)  94 us
    reduce_scatter x1, waiting for transfers between devices, shards(): lax.psum_scatter(grad_value, 'row', scatter_dimension=0, tiled=True)  61.6 us
    reduce_scatter x1, waiting for transfers between devices, shards(): lax.psum_scatter(grad_key, 'row', scatter_dimension=0, tiled=True)  61.5 us
    ppermute x3, waiting for transfers between devices, grow_blocks(): lax.ppermute(tiles, axis, [(i, i ^ distance) for i in range(devices)])  53.1 us
    reduce_scatter x1, waiting for transfers between devices, shards(): lax.psum_scatter(grad_gate, 'row', scatter_dimension=0, tiled=True)  48.4 us
  transfers between devices with their start and end apart: 24, of which 20 were waited for; matrix products, arithmetic and copies ran while one was open for 14% of the time, Pallas kernels for 0%

profile of v1, /device:TPU:0, one launch (start us, length us, event | category | flops | bytes accessed | tf_op | source)
XLA Modules:
  0.0 1449.4 jit_solution(1018670565512623835)
XLA Ops:
  16.0 24.8 %all_gather.33 = bf16[1152,192]{1,0:T(8,128)(2,1)S(1)} all-gather(bf16[72,192]{1,0:T(8,128)(2,1)S(1)} %copy-done.41), channel_id=1, replica_groups=mesh['row'=16,'col'=2] {'row'}, dimensions={0}, use_global_device_ids=true | all-gather | bytes 470016 | tf_op jit(solution)/shard_map/all_gather | solution.py:115
  40.9 19.0 %all_gather.31 = bf16[1152,192]{1,0:T(8,128)(2,1)S(1)} all-gather(bf16[72,192]{1,0:T(8,128)(2,1)S(1)} %copy-done.42), channel_id=1, replica_groups=mesh['row'=16,'col'=2] {'row'}, dimensions={0}, use_global_device_ids=true | all-gather | bytes 470016 | tf_op jit(solution)/shard_map/all_gather | solution.py:116
  63.7 12.0 all_gather.34
  77.6 11.2 all_gather.32
  99.9 6.8 fusion.73
  106.7 7.6 all-to-all-done
  115.5 11.3 fusion.64
  126.8 55.4 %while.50 = (s32[]{:T(128)}, bf16[6,512,192]{1,2,0:T(8,128)(2,1)}, f32[6,3,512]{2,1,0:T(4,128)}, s32[6]{0:T(128)S(1)}, bf16[1024,384]{0,1:T(8,128)(2,1)S(1)}, /*...) while((s32[]{:T(128)}, bf16[6,512,192]{1,2,0:T(8,128)(2,1)}, ...), condition=%wide.region_6.7_spmd.clone.clone, body=%wide.region_3.6_spmd.clone.sunk.clone | while | flops 418380288 | bytes 22482160 | solution.py:190
  182.1 18.5 %all_to_all.64 = bf16[512,2,576]{0,2,1:T(8,128)(2,1)S(1)} all-to-all(bf16[512,2,576]{0,2,1:T(8,128)(2,1)} %bitcast.292), channel_id=1, replica_groups=mesh['row'=16,'col'=2] {'col'}, dimensions={1} | all-to-all | bytes 2359296 | tf_op jit(solution)/shard_map/all_to_all | solution.py:75
  200.8 6.2 fusion.125
  210.2 77.8 %reduce-scatter.18.cloned.1.call-done = f32[512,1152]{1,0:T(8,128)} async-done(((f32[1024,1152]{1,0:T(8,128)}), f32[512,1152]{1,0:T(8,128)}) %reduce-scatter.18.cloned.1.call-update) | async-done | bytes 2359312 | tf_op jit(solution)/shard_map/reduce_scatter | solution.py:79
  294.6 25.7 %collective-permute-done = bf16[1,512,1152]{2,1,0:T(8,128)(2,1)} collective-permute-done((bf16[1,512,1152]{2,1,0:T(8,128)(2,1)}, bf16[1,512,1152]{2,1,0:T(8,128)(2,1)}, u32[]{:S(2)}, u32[]{:S(2)}) %collective-permute-start) | collective-permute-done | bytes 1179680 | tf_op jit(solution)/shard_map/ppermute | solution.py:26
  325.0 10.6 all-gather.13.cloned.1.call-done
  335.5 9.6 fusion.126
  345.1 39.0 %all-gather.15.cloned.1.call-done = bf16[1152,1536]{1,0:T(8,128)(2,1)} async-done(((bf16[72,1536]{1,0:T(8,128)(2,1)}), bf16[1152,1536]{1,0:T(8,128)(2,1)}) %all-gather.15.cloned.1.call-update) | async-done | bytes 3538960 | tf_op jit(solution)/shard_map/all_gather | solution.py:119
  384.1 9.6 fusion.127
  393.8 39.1 %all-gather.17.cloned.1.call-done = bf16[1536,1152]{0,1:T(8,128)(2,1)} async-done(((bf16[1536,72]{0,1:T(8,128)(2,1)}), bf16[1536,1152]{0,1:T(8,128)(2,1)}) %all-gather.17.cloned.1.call-update) | async-done | bytes 3538960 | tf_op jit(solution)/shard_map/all_gather | solution.py:120
  432.9 12.7 multiply_convert_fusion
  445.6 4.2 fusion.129
  449.9 6.1 convolution_add_fusion.2
  456.6 9.4 fusion.128
  466.0 49.2 %reduce-scatter.22.cloned.1.call-done = f32[512,1152]{1,0:T(8,128)} async-done(((f32[1024,1152]{1,0:T(8,128)}), f32[512,1152]{1,0:T(8,128)}) %reduce-scatter.22.cloned.1.call-update) | async-done | bytes 2359312 | tf_op jit(solution)/shard_map/reduce_scatter | solution.py:79
  518.0 59.5 %reduce-scatter.20.cloned.1.call-done = f32[512,1152]{1,0:T(8,128)} async-done(((f32[1024,1152]{1,0:T(8,128)}), f32[512,1152]{1,0:T(8,128)}) %reduce-scatter.20.cloned.1.call-update) | async-done | bytes 2359312 | tf_op jit(solution)/shard_map/reduce_scatter | solution.py:79
  577.5 4.5 convert_bitcast_fusion.1
  582.5 27.4 %collective-permute-done.2 = bf16[1,512,1152]{2,1,0:T(8,128)(2,1)S(1)} collective-permute-done((bf16[1,512,1152]{2,1,0:T(8,128)(2,1)S(1)}, bf16[1,512,1152]{2,1,0:T(8,128)(2,1)S(1)}, u32[]{:S(2)}, u32[]{:S(2)}) %collective-permute-start.2) | collective-permute-done | bytes 1179680 | tf_op jit(solution)/shard_map/ppermute | solution.py:26
  618.2 14.1 all-to-all-done.2
  635.1 125.2 %while.51 = (s32[]{:T(128)}, f32[1024,384]{0,1:T(8,128)}, f32[1024,384]{0,1:T(8,128)}, f32[6,512,192]{1,2,0:T(8,128)}, s32[6]{0:T(128)S(1)}, /*index=5*/bf16[102...) while((s32[]{:T(128)}, f32[1024,384]{0,1:T(8,128)}, ...), condition=%wide.region_15.16_spmd.clone.clone, body=%wide.region_13.15_spmd.clone.sunk.clone | while | flops 1027209728 | bytes 67165064 | solution.py:287
  760.3 6.5 fusion.70
  768.2 6.8 fusion.74
  776.0 8.0 fusion.51
  786.4 8.7 subtract_convert_fusion
  795.1 17.6 %all_to_all.65 = bf16[512,2,576]{0,2,1:T(8,128)(2,1)S(1)} all-to-all(bf16[512,2,576]{0,2,1:T(8,128)(2,1)S(1)} %subtract_convert_fusion), channel_id=1, replica_groups=mesh['row'=16,'col'=2] {'col'}, dimensions={1} | all-to-all | bytes 2359296 | tf_op jit(solution)/shard_map/all_to_all | solution.py:75
  813.9 4.4 fusion.130
  818.4 5.7 convolution_add_fusion.1
  824.1 6.7 reduce-scatter.26.cloned.1.call-done
  830.8 5.7 convolution_add_fusion
  838.1 7.5 fusion.132
  845.8 7.6 fusion.133
  855.0 7.7 fusion.134
  882.0 14.7 %reduce-scatter.28.cloned.1.call-done = f32[512,1152]{1,0:T(8,128)} async-done(((f32[1024,1152]{1,0:T(8,128)}), f32[512,1152]{1,0:T(8,128)}) %reduce-scatter.28.cloned.1.call-update) | async-done | bytes 2359312 | tf_op jit(solution)/shard_map/reduce_scatter | solution.py:79
  899.6 39.7 %all-reduce.2 = (f32[1152]{0:T(1024)}, f32[1152]{0:T(1024)}) all-reduce(f32[1152]{0:T(1024)} %get-tuple-element.251, f32[1152]{0:T(1024)S(1)} %copy-done.43), channel_id=1, replica_groups=mesh['row'=16,'col'=2] {'row','col'}, use_global_device_ids=true, to_apply=%region_21.22 | all-reduce | flops 2304 | bytes 18432 | tf_op jit(solution)/shard_map/psum | solution.py:344
  943.3 48.4 %reduce-scatter.34.cloned.1.call-done = f32[72,1536]{1,0:T(8,128)} async-done(((f32[1152,1536]{1,0:T(8,128)}), f32[72,1536]{1,0:T(8,128)}) %reduce-scatter.34.cloned.1.call-update) | async-done | bytes 442384 | tf_op jit(solution)/shard_map/reduce_scatter | solution.py:340
  991.8 94.6 %reduce-scatter.36.cloned.1.call-done = f32[72,1536]{1,0:T(8,128)} async-done(((f32[1152,1536]{1,0:T(8,128)}), f32[72,1536]{1,0:T(8,128)}) %reduce-scatter.36.cloned.1.call-update) | async-done | bytes 442384 | tf_op jit(solution)/shard_map/reduce_scatter | solution.py:341
  1086.4 94.0 %reduce-scatter.38.cloned.1.call-done = f32[1536,72]{0,1:T(8,128)} async-done(((f32[1536,1152]{0,1:T(8,128)}), f32[1536,72]{0,1:T(8,128)}) %reduce-scatter.38.cloned.1.call-update) | async-done | bytes 442384 | tf_op jit(solution)/shard_map/reduce_scatter | solution.py:342
  1180.4 69.7 %reduce-scatter.42.cloned.1.call-done = f32[576,72]{0,1:T(8,128)} async-done(((f32[576,1152]{0,1:T(8,128)}), f32[576,72]{0,1:T(8,128)}) %reduce-scatter.42.cloned.1.call-update) | async-done | bytes 165904
  1250.0 61.5 %reduce-scatter.30.cloned.1.call-done = f32[72,192]{1,0:T(8,128)} async-done(((f32[1152,192]{1,0:T(8,128)}), f32[72,192]{1,0:T(8,128)}) %reduce-scatter.30.cloned.1.call-update) | async-done | bytes 55312 | tf_op jit(solution)/shard_map/reduce_scatter | solution.py:337
  1311.6 61.6 %reduce-scatter.32.cloned.1.call-done = f32[72,192]{1,0:T(8,128)} async-done(((f32[1152,192]{1,0:T(8,128)}), f32[72,192]{1,0:T(8,128)}) %reduce-scatter.32.cloned.1.call-update) | async-done | bytes 55312 | tf_op jit(solution)/shard_map/reduce_scatter | solution.py:338
  1373.2 69.3 %reduce-scatter.40.cloned.1.call-done = f32[72,576]{1,0:T(8,128)} async-done(((f32[1152,576]{1,0:T(8,128)}), f32[72,576]{1,0:T(8,128)}) %reduce-scatter.40.cloned.1.call-update) | async-done | bytes 165904
  (394 shorter events, 255.0 us)
Async XLA Ops:
  7.2 8.8 copy-start.41
  7.2 33.7 %copy-start.42 = (bf16[72,192]{1,0:T(8,128)(2,1)S(1)}, bf16[72,192]{1,0:T(8,128)(2,1)}, u32[]{:S(2)}) copy-start(bf16[72,192]{1,0:T(8,128)(2,1)} %param.22) | copy-start | bytes 82948
  7.2 52.7 %copy-start.31 = (s32[1024]{0:T(1024)S(1)}, s32[1024]{0:T(1024)}, u32[]{:S(2)}) copy-start(s32[1024]{0:T(1024)} %param.28) | copy-start | bytes 12292
  7.2 52.8 %all-gather.7.cloned.1.call-start = ((), (), s32[]{:S(2)}) async-start(), calls=%async_computation.17 | async-start | bytes 3538944 | tf_op jit(solution)/shard_map/all_gather | solution.py:111
  8.0 82.0 %all-gather.9.cloned.1.call-start = ((), (), s32[]{:S(2)}) async-start(), calls=%async_computation.18 | async-start | bytes 1566720 | tf_op jit(solution)/shard_map/all_gather | solution.py:114
  8.7 192.1 %all-gather.11.cloned.1.call-start = ((), (), s32[]{:S(2)}) async-start(), calls=%async_computation.19 | async-start | bytes 1566720 | tf_op jit(solution)/shard_map/all_gather | solution.py:117
  13.0 77.0 %copy-start.37 = (f32[1152]{0:T(1024)}, f32[1152]{0:T(1024)S(1)}, u32[]{:S(2)}) copy-start(f32[1152]{0:T(1024)S(1)} %convert_element_type.125) | copy-start | bytes 13828
  40.9 21.5 %copy-start.22 = (bf16[1152,192]{1,0:T(8,128)(2,1)}, bf16[1152,192]{1,0:T(8,128)(2,1)S(1)}, u32[]{:S(2)}) copy-start(bf16[1152,192]{1,0:T(8,128)(2,1)S(1)} %all_gather.33) | copy-start | bytes 1327108
  59.9 16.6 %copy-start.20 = (bf16[1152,192]{1,0:T(8,128)(2,1)}, bf16[1152,192]{1,0:T(8,128)(2,1)S(1)}, u32[]{:S(2)}) copy-start(bf16[1152,192]{1,0:T(8,128)(2,1)S(1)} %all_gather.31) | copy-start | bytes 1327108
  62.5 27.4 %copy-start.53 = (f32[1024]{0:T(1024)}, f32[1024]{0:T(1024)S(1)}, u32[]{:S(2)}) copy-start(f32[1024]{0:T(1024)S(1)} %add_rsqrt_fusion) | copy-start | bytes 12292
  95.0 19.3 %all-to-all-start = ((bf16[2,512,576]{1,2,0:T(8,128)(2,1)}), bf16[2,512,576]{1,2,0:T(8,128)(2,1)S(1)}, u32[]{:S(2)}, u32[]{:S(2)}) async-start(bf16[2,512,576]{1,2,0:T(8,128)(2,1)} %bitcast.179), calls=%async_computation | async-start | bytes 2359296 | tf_op jit(solution)/shard_map/all_to_all | solution.py:71
  98.7 189.3 %reduce-scatter.18.cloned.1.call-start = ((), (), s32[]{:S(2)}) async-start(), calls=%async_computation.20 | async-start | bytes 7077888 | tf_op jit(solution)/shard_map/reduce_scatter | solution.py:79
  182.1 18.6 %copy-start.12 = (bf16[1024,384]{0,1:T(8,128)(2,1)}, bf16[1024,384]{0,1:T(8,128)(2,1)S(1)}, u32[]{:S(2)}) copy-start(bf16[1024,384]{0,1:T(8,128)(2,1)S(1)} %get-tuple-element.718) | copy-start | bytes 2359300
  182.1 24.8 %copy-start.9 = (bf16[1024,384]{0,1:T(8,128)(2,1)}, bf16[1024,384]{0,1:T(8,128)(2,1)S(1)}, u32[]{:S(2)}) copy-start(bf16[1024,384]{0,1:T(8,128)(2,1)S(1)} %get-tuple-element.693) | copy-start | bytes 2359300
  200.8 6.2 copy-start.24
  207.0 81.0 %copy-start.7 = (bf16[512,1152]{1,0:T(8,128)(2,1)S(1)}, bf16[512,1152]{1,0:T(8,128)(2,1)}, u32[]{:S(2)}) copy-start(bf16[512,1152]{1,0:T(8,128)(2,1)} %param.17) | copy-start | bytes 3538948
  207.0 128.5 %all-gather.13.cloned.1.call-start = ((), (), s32[]{:S(2)}) async-start(), calls=%async_computation.21 | async-start | bytes 3760128 | tf_op jit(solution)/shard_map/all_gather | solution.py:118
  207.6 176.5 %all-gather.15.cloned.1.call-start = ((), (), s32[]{:S(2)}) async-start(), calls=%async_computation.22 | async-start | bytes 3760128 | tf_op jit(solution)/shard_map/all_gather | solution.py:119
  208.2 224.7 %all-gather.17.cloned.1.call-start = ((), (), s32[]{:S(2)}) async-start(), calls=%async_computation.23 | async-start | bytes 3760128 | tf_op jit(solution)/shard_map/all_gather | solution.py:120
  208.9 306.2 %reduce-scatter.22.cloned.1.call-start = ((), (), s32[]{:S(2)}) async-start(), calls=%async_computation.25 | async-start | bytes 7077888 | tf_op jit(solution)/shard_map/reduce_scatter | solution.py:79
  209.2 83.5 %collective-permute-start.1 = (bf16[1,512,1152]{2,1,0:T(8,128)(2,1)}, bf16[1,512,1152]{2,1,0:T(8,128)(2,1)}, u32[]{:S(2)}, u32[]{:S(2)}) collective-permute-start(bf16[1,512,1152]{2,1,0:T(8,128)(2,1)} %bitcast.13), channel_id=1, source_target_pairs={{0,1},{1,0},{2,3},{3,2},{4,5},{5,4},{6,7},{7,6},{8,9},{9,8},{10,11... | collective-permute-start | bytes 3538952 | tf_op jit(solution)/shard_map/ppermute | solution.py:26
  292.1 28.2 %collective-permute-start = (bf16[1,512,1152]{2,1,0:T(8,128)(2,1)}, bf16[1,512,1152]{2,1,0:T(8,128)(2,1)}, u32[]{:S(2)}, u32[]{:S(2)}) collective-permute-start(bf16[1,512,1152]{2,1,0:T(8,128)(2,1)} %get-tuple-element.319), channel_id=1, source_target_pairs={{0,1},{1,0},{2,3},{3,2},{4,5},{5,4},{6,7},{7,6},{8,9},{9,8},{10,11... | collective-permute-start | bytes 3538952 | tf_op jit(solution)/shard_map/ppermute | solution.py:26
  432.9 12.7 copy-start.57
  456.0 121.5 %reduce-scatter.20.cloned.1.call-start = ((), (), s32[]{:S(2)}) async-start(), calls=%async_computation.24 | async-start | bytes 7077888 | tf_op jit(solution)/shard_map/reduce_scatter | solution.py:79
  465.9 49.2 %copy-start.33 = (f32[1152]{0:T(1024)S(1)}, f32[1152]{0:T(1024)}, u32[]{:S(2)}) copy-start(f32[1152]{0:T(1024)} %convert_element_type.142) | copy-start | bytes 13828
  465.9 49.2 %copy-start.47 = (f32[512]{0:T(512)S(1)}, f32[512]{0:T(512)}, u32[]{:S(2)}) copy-start(f32[512]{0:T(512)} %copy-done.46) | copy-start | bytes 6148
  582.0 28.1 %copy-start.5 = (f32[512,1152]{1,0:T(8,128)}, f32[512,1152]{1,0:T(8,128)S(1)}, u32[]{:S(2)}) copy-start(f32[512,1152]{1,0:T(8,128)S(1)} %get-tuple-element.306) | copy-start | bytes 7077892
  582.1 27.8 %collective-permute-start.2 = (bf16[1,512,1152]{2,1,0:T(8,128)(2,1)S(1)}, bf16[1,512,1152]{2,1,0:T(8,128)(2,1)S(1)}, u32[]{:S(2)}, u32[]{:S(2)}) collective-permute-start(bf16[1,512,1152]{2,1,0:T(8,128)(2,1)S(1)} %convert_bitcast_fusion), channel_id=1, source_target_pairs={{0,1},{1,0},{2,3},{3,2},{4,5},{5,4},{6,7},{7,6},{8,9},{9,8},{10,11... | collective-permute-start | bytes 3538952 | tf_op jit(solution)/shard_map/ppermute | solution.py:26
  614.4 18.0 %all-to-all-start.2 = ((bf16[2,512,576]{1,2,0:T(8,128)(2,1)}), bf16[2,512,576]{1,2,0:T(8,128)(2,1)S(1)}, u32[]{:S(2)}, u32[]{:S(2)}) async-start(bf16[2,512,576]{1,2,0:T(8,128)(2,1)} %bitcast.178), calls=%async_computation.5 | async-start | bytes 2359296 | tf_op jit(solution)/shard_map/all_to_all | solution.py:71
  618.0 200.4 %reduce-scatter.24.cloned.1.call-start = ((), (), s32[]{:S(2)}) async-start(), calls=%async_computation.26 | async-start | bytes 2359296 | tf_op jit(solution)/shard_map/reduce_scatter | solution.py:309
  635.1 125.2 %copy-start.36 = (f32[1024]{0:T(1024)S(1)}, f32[1024]{0:T(1024)}, u32[]{:S(2)}) copy-start(f32[1024]{0:T(1024)} %copy-done.34) | copy-start | bytes 12292
  635.1 125.2 %copy-start.45 = (f32[384]{0:T(512)S(1)}, f32[384]{0:T(512)}, u32[]{:S(2)}) copy-start(f32[384]{0:T(512)} %fusion.100) | copy-start | bytes 4612
  768.2 7.2 copy-start.17
  775.0 55.7 %reduce-scatter.26.cloned.1.call-start = ((), (), s32[]{:S(2)}) async-start(), calls=%async_computation.27 | async-start | bytes 2359296 | tf_op jit(solution)/shard_map/reduce_scatter | solution.py:310
  776.0 8.0 copy-start.3
  784.1 112.5 %reduce-scatter.28.cloned.1.call-start = ((), (), s32[]{:S(2)}) async-start(), calls=%async_computation.28 | async-start | bytes 7077888 | tf_op jit(solution)/shard_map/reduce_scatter | solution.py:79
  795.1 18.8 %copy-start.59 = (bf16[1152,576]{1,0:T(8,128)(2,1)S(1)}, bf16[1152,576]{1,0:T(8,128)(2,1)}, u32[]{:S(2)}) copy-start(bf16[1152,576]{1,0:T(8,128)(2,1)} %all-gather.9.cloned.1.call-done) | copy-start | bytes 3981316
  818.4 12.4 copy-start.21
  836.5 155.3 %reduce-scatter.34.cloned.1.call-start = ((), (), s32[]{:S(2)}) async-start(), calls=%async_computation.31 | async-start | bytes 7520256 | tf_op jit(solution)/shard_map/reduce_scatter | solution.py:340
  845.7 240.7 %reduce-scatter.36.cloned.1.call-start = ((), (), s32[]{:S(2)}) async-start(), calls=%async_computation.32 | async-start | bytes 7520256 | tf_op jit(solution)/shard_map/reduce_scatter | solution.py:341
  853.4 327.0 %reduce-scatter.38.cloned.1.call-start = ((), (), s32[]{:S(2)}) async-start(), calls=%async_computation.33 | async-start | bytes 7520256 | tf_op jit(solution)/shard_map/reduce_scatter | solution.py:342
  862.7 387.3 %reduce-scatter.42.cloned.1.call-start = ((), (), s32[]{:S(2)}) async-start(), calls=%async_computation.35 | async-start | bytes 3133440
  868.4 443.2 %reduce-scatter.30.cloned.1.call-start = ((), (), s32[]{:S(2)}) async-start(), calls=%async_computation.29 | async-start | bytes 1253376 | tf_op jit(solution)/shard_map/reduce_scatter | solution.py:337
  873.3 499.9 %reduce-scatter.32.cloned.1.call-start = ((), (), s32[]{:S(2)}) async-start(), calls=%async_computation.30 | async-start | bytes 1253376 | tf_op jit(solution)/shard_map/reduce_scatter | solution.py:338
  876.6 565.8 %reduce-scatter.40.cloned.1.call-start = ((), (), s32[]{:S(2)}) async-start(), calls=%async_computation.34 | async-start | bytes 3133440
  880.6 16.1 %copy-start.8 = (bf16[512,1152]{1,0:T(8,128)(2,1)S(1)}, bf16[512,1152]{1,0:T(8,128)(2,1)}, u32[]{:S(2)}) copy-start(bf16[512,1152]{1,0:T(8,128)(2,1)} %param.17) | copy-start | bytes 3538948
  880.6 19.0 %copy-start.43 = (f32[1152]{0:T(1024)S(1)}, f32[1152]{0:T(1024)}, u32[]{:S(2)}) copy-start(f32[1152]{0:T(1024)} %get-tuple-element.249) | copy-start | bytes 13828
  880.6 59.4 %copy-start.6 = (f32[512,1152]{1,0:T(8,128)S(1)}, f32[512,1152]{1,0:T(8,128)}, u32[]{:S(2)}) copy-start(f32[512,1152]{1,0:T(8,128)} %copy-done.5) | copy-start | bytes 7077892
  (59 other events, 160.1 us)
Sparse Core Ops, SparseCore 0:
  9.6 38.7 all-gather.6
  50.6 39.3 all-gather.8
  92.1 38.1 all-gather.10
  207.1 80.7 reduce-scatter.17
  290.3 45.1 all-gather.12
  337.9 46.1 all-gather.14
  386.7 46.1 all-gather.16
  456.1 59.0 reduce-scatter.21
  517.5 59.9 reduce-scatter.19
  775.1 26.9 reduce-scatter.23
  804.4 26.3 reduce-scatter.25
  836.6 59.9 reduce-scatter.27
  901.2 90.5 reduce-scatter.33
  996.8 89.5 reduce-scatter.35
  1090.8 89.5 reduce-scatter.37
  1185.2 64.7 reduce-scatter.41
  1254.5 57.0 reduce-scatter.29
  1316.1 57.0 reduce-scatter.31
  1378.2 64.2 reduce-scatter.39
